TPU v7x, 32 devices: a whole 2x2x4 slice. The times are simulated.
32 devices in a mesh: group: 2 (over y), tm: 4 (over x, core), row: 4 (over z).
Axes of the slice: x: 2, y: 2, z: 4, core: 2. Of those that a mesh axis runs over, the one named last changes fastest.
Arguments:
- traces: bfloat16 [4096, 1024], P('row', ('group', 'tm')), parts along dimension 1, may hold values from -6 to 6
- weights: bfloat16 [4, 4096, 4096], P(None, 'row'), may hold values from -0.09375 to 0.09375
- pattern: int32 [4, 32, 32], replicated, may hold values 0 or 1
- cluster: int32 [4096], replicated, may hold values from 0 to 31
- element_damping_rate: float32 [4096], replicated, may hold values from 0 to 0.034, as said below
- local_step_length: float32 [512], P('tm'), may hold values from 0.4 to 1.9, as said below
- housing_keep_share: float32 [512], P('tm'), may hold values from 0.2 to 1, as said below
- admittance: float32 [4096], replicated, may hold values from 0.5 to 2
Outputs:
- adjoint_state: float32 [4096, 1024], P('row', ('group', 'tm')), parts along dimension 1
- pressure: bfloat16 [4096, 1024], P('row', ('group', 'tm')), parts along dimension 1
There are 2 independent parts, one for each index of `group`. A program takes and returns all parts, laid end to end along the dimension named above; an argument that names none is the same for every part. Nothing has to cross between parts.
Inputs may be any that keep to these rules, and one draw needn't show every extreme that they name: `element_damping_rate`: damping rates, positive. `local_step_length`: positive step lengths. `housing_keep_share`: kept shares, positive.
All inputs are finite; a program needn't handle non-finite values.
Results may differ from a plain program's by a relative error of at most 0.012.
Values may be sent and summed in bfloat16 or wider, within the bound.
No kernel may reach another device: no remote copies, remote signals or barrier semaphores. Data moves between devices by JAX's collectives and lax.ppermute only.
A program may use at most 192 MiB of HBM per device.

v0:
```python
import jax
import jax.numpy as jnp
from jax import lax
from jax.sharding import PartitionSpec as P


def carried_in(array, axis, join, neutral):
    count = lax.axis_size(axis)
    place = lax.axis_index(axis)
    ahead = count - 1 - place
    gathered = jax.tree.map(
        lambda a, kind: lax.all_gather(a.astype(kind), axis),
        array,
        jax.tree.map(lambda a: jnp.bfloat16 if a.dtype == jnp.float32 else a.dtype, array),
    )
    state = jax.tree.map(lambda a, e: jnp.zeros_like(a) + jnp.asarray(e, a.dtype), array, neutral)

    def one(hop, state):
        source = count - 1 - hop
        return join(
            state,
            jax.tree.map(
                lambda a, own: lax.dynamic_index_in_dim(a, source, 0, False).astype(own.dtype),
                gathered,
                array,
            ),
        )

    return lax.fori_loop(0, ahead, one, state)


def from_behind(array, axis, by):
    count = lax.axis_size(axis)
    pairs = [(i, i + by) for i in range(count) if 0 <= i + by < count]
    return lax.ppermute(array, axis, pairs)


def lag_kernels(weights, pattern, cluster, first_row):
    local_rows = weights.shape[1]
    own_labels = lax.dynamic_slice_in_dim(cluster, first_row, local_rows, 0)
    labels = jnp.arange(pattern.shape[1], dtype=jnp.int32)
    row_onehot = (own_labels[:, None] == labels[None, :]).astype(jnp.bfloat16)
    column_onehot = (labels[:, None] == cluster[None, :]).astype(jnp.bfloat16)
    kernels = []
    for lag_index in range(weights.shape[0]):
        picked = jnp.dot(
            row_onehot, pattern[lag_index].astype(jnp.bfloat16), preferred_element_type=jnp.float32
        )
        table = jnp.dot(
            picked.astype(jnp.bfloat16), column_onehot, preferred_element_type=jnp.float32
        )
        kernels.append(weights[lag_index] * table.astype(jnp.bfloat16))
    return kernels


def correlate(kernels, extended):
    length = extended.shape[1] - len(kernels) + 1
    running = None
    for lag_index in range(len(kernels)):
        columns = kernels[lag_index]
        product_term = lax.dot_general(
            columns,
            extended[:, lag_index : lag_index + length],
            (((0,), (0,)), ((), ())),
            preferred_element_type=jnp.float32,
        )
        running = product_term if running is None else running + product_term
    return running


def reconstruct(kernels, extended, running):
    number_of_lags = len(kernels)
    length = extended.shape[1] - number_of_lags + 1
    col_count = extended.shape[0]
    for lag_index in range(number_of_lags):
        columns = lax.slice_in_dim(kernels[lag_index], 0, col_count, axis=1)
        offset = number_of_lags - 1 - lag_index
        running = running + jnp.dot(
            columns, extended[:, offset : offset + length], preferred_element_type=jnp.float32
        )
    return running


def chain_step(earlier, later):
    return (later[0] * earlier[0], later[1] + later[0] * earlier[1])


def block_recurrence(keep_fraction, inflow):
    elements = keep_fraction.shape[0]
    length = keep_fraction.shape[1]
    span = 8
    keep_rows = keep_fraction.T.reshape(length // span, span, elements)
    inflow_rows = inflow.T.reshape(length // span, span, elements)

    def advance(carry, pieces):
        kept_now, state_now = carry
        keep_block, inflow_block = pieces
        kept_list = [None] * span
        state_list = [None] * span
        for inner in range(span - 1, -1, -1):
            state_now = keep_block[inner] * state_now + inflow_block[inner]
            kept_now = keep_block[inner] * kept_now
            kept_list[inner] = kept_now
            state_list[inner] = state_now
        return ((kept_now, state_now), (jnp.stack(kept_list, 0), jnp.stack(state_list, 0)))

    start = (jnp.ones((elements,), jnp.float32), jnp.zeros((elements,), jnp.float32))
    _, outputs = lax.scan(advance, start, (keep_rows, inflow_rows), reverse=True)
    retained = outputs[0].reshape(length, elements).T
    partial_state = outputs[1].reshape(length, elements).T
    return (retained, partial_state)


def forward_step(
    adjoint_total_sum,
    element_damping_rate,
    local_step_length,
    housing_keep_share,
    admittance,
    number_of_lags,
):
    length = adjoint_total_sum.shape[1]
    distribute_rows = element_damping_rate[:, None] * local_step_length[None, :]
    keep_fraction = jnp.exp(-distribute_rows) * housing_keep_share[None, :]
    inflow = jnp.sqrt(-jnp.expm1(-2.0 * distribute_rows)) * adjoint_total_sum
    retained, partial_state = block_recurrence(keep_fraction, inflow)
    neutral = (jnp.ones_like(retained[:, 0]), jnp.zeros_like(partial_state[:, 0]))
    incoming = carried_in((retained[:, 0], partial_state[:, 0]), "tm", chain_step, neutral)
    adj_state = partial_state + retained * incoming[1][:, None]
    driving = (admittance[:, None] * adj_state).astype(jnp.bfloat16)
    leading = from_behind(driving[:, length - number_of_lags + 1 :], "tm", 1)
    return (adj_state, jnp.concatenate([leading, driving], 1))


def local(
    traces,
    weights,
    pattern,
    cluster,
    element_damping_rate,
    local_step_length,
    housing_keep_share,
    admittance,
):
    local_rows = traces.shape[0]
    length = traces.shape[1]
    number_of_lags = weights.shape[0]
    first_row = lax.axis_index("row") * local_rows
    kernels = lag_kernels(weights, pattern, cluster, first_row)
    trailing = from_behind(traces[:, : number_of_lags - 1], "tm", -1)
    extended = jnp.concatenate([traces, trailing], 1)
    empty = jnp.zeros((local_rows, length), jnp.float32)
    adjoint_total_sum = lax.psum(correlate(kernels, extended).astype(jnp.bfloat16), "row").astype(
        jnp.float32
    )
    adj_state, driving = forward_step(
        adjoint_total_sum,
        element_damping_rate,
        local_step_length,
        housing_keep_share,
        admittance,
        number_of_lags,
    )
    pressure = reconstruct(kernels, driving, empty)
    adj_state = lax.dynamic_slice_in_dim(adj_state, first_row, local_rows, 0)
    return (adj_state, pressure.astype(jnp.bfloat16))


def solution(mesh):
    placed = (P("row", ("group", "tm")), P(None, "row", None), P(), P(), P(), P("tm"), P("tm"), P())
    return jax.shard_map(
        local,
        mesh=mesh,
        in_specs=placed,
        out_specs=(P("row", ("group", "tm")), P("row", ("group", "tm"))),
        check_vma=False,
    )
```

profile of v0, /device:TPU:1, one launch (start us, length us, event | category | flops | bytes accessed | tf_op | source)
XLA Modules:
  0.0 235.5 jit_solution(9270569396340060062)
XLA Ops:
  7.2 2.0 collective-permute-start
  10.7 8.1 %bitcast_multiply_fusion.3 = bf16[1024,4096]{1,0:T(8,128)(2,1)} fusion(bf16[4,1024,4096]{2,1,0:T(8,128)(2,1)} %param.13, s32[4096]{0:T(1024)} %param.15, s32[1024]{0:T(1024)S(1)} %dynamic_slice.40, bf16[4,32,32]{2,1,0:T(8,128)(2,1)S(1)} %convert.14), kind=kOutput, calls=%fused_computation.34 | convolution fusion | flops 291700736 | bytes 16805888 | tf_op jit(solution)/shard_map/dot_general | solution.py:49
  18.8 7.2 %bitcast_multiply_fusion.2 = bf16[1024,4096]{1,0:T(8,128)(2,1)} fusion(bf16[4,1024,4096]{2,1,0:T(8,128)(2,1)} %param.13, s32[4096]{0:T(1024)S(1)} %copy-done.2, s32[1024]{0:T(1024)S(1)} %dynamic_slice.40, bf16[4,32,32]{2,1,0:T(8,128)(2,1)S(1)} %convert.14), kind=kOutput, calls=%fused_computation.33 | convolution fusion | flops 291700736 | bytes 16805888 | tf_op jit(solution)/shard_map/dot_general | solution.py:49
  26.0 7.1 %bitcast_multiply_fusion = bf16[1024,4096]{1,0:T(8,128)(2,1)} fusion(bf16[4,1024,4096]{2,1,0:T(8,128)(2,1)} %param.13, s32[4096]{0:T(1024)S(1)} %copy-done.2, s32[1024]{0:T(1024)S(1)} %dynamic_slice.40, bf16[4,32,32]{2,1,0:T(8,128)(2,1)S(1)} %convert.14), kind=kOutput, calls=%fused_computation.31 | convolution fusion | flops 291700736 | bytes 16805888 | tf_op jit(solution)/shard_map/dot_general | solution.py:49
  33.1 7.2 %bitcast_multiply_fusion.1 = bf16[1024,4096]{1,0:T(8,128)(2,1)} fusion(bf16[4,1024,4096]{2,1,0:T(8,128)(2,1)} %param.13, s32[4096]{0:T(1024)S(1)} %copy-done.2, s32[1024]{0:T(1024)S(1)} %dynamic_slice.40, bf16[4,32,32]{2,1,0:T(8,128)(2,1)S(1)} %convert.14), kind=kOutput, calls=%fused_computation.32 | convolution fusion | flops 291700736 | bytes 16805888 | tf_op jit(solution)/shard_map/dot_general | solution.py:49
  40.3 6.0 %fusion.42 = f32[4096,128]{1,0:T(8,128)S(1)} fusion(bf16[1024,4096]{1,0:T(8,128)(2,1)} %bitcast_multiply_fusion.3, bf16[1024,128]{1,0:T(8,128)(2,1)S(1)} %copy-done.1), kind=kOutput, calls=%fused_computation.94 | convolution fusion | flops 1073741824 | bytes 10747904 | tf_op jit(solution)/shard_map/dot_general | solution.py:61
  46.4 2.6 %fusion.20 = f32[4096,128]{1,0:T(8,128)S(1)} fusion(bf16[1024,4096]{1,0:T(8,128)(2,1)S(1)} %copy-done, bf16[1024,131]{1,0:T(8,128)(2,1)S(1)} %constant_dynamic-update-slice_fusion), kind=kOutput, calls=%fused_computation.72 | convolution fusion | flops 1073741824 | bytes 10747904 | tf_op jit(solution)/shard_map/dot_general | solution.py:61
  49.0 2.5 %convolution_add_fusion.1 = f32[4096,128]{1,0:T(8,128)S(1)} fusion(f32[4096,128]{1,0:T(8,128)S(1)} %fusion.42, bf16[1024,4096]{1,0:T(8,128)(2,1)S(1)} %bitcast.168, bf16[1024,131]{1,0:T(8,128)(2,1)S(1)} %constant_dynamic-update-slice_fusion), kind=kOutput, calls=%fused_computation.37 | convolution fusion | flops 1074266112 | bytes 12845056 | tf_op jit(solution)/shard_map/dot_general | solution.py:61
  51.7 3.6 %fusion.2 = bf16[4096,128]{1,0:T(8,128)(2,1)} fusion(f32[4096,128]{1,0:T(8,128)S(1)} %fusion.20, f32[4096,128]{1,0:T(8,128)S(1)} %convolution_add_fusion.1, bf16[1024,4096]{1,0:T(8,128)(2,1)S(1)} %bitcast.170, bf16[1024,131]{1,0:T(8,128)(2,1)S(1)} %constant_dynamic-update-slice_fusion), kind=kOutput, calls=%fused_computation.38 | convolution fusion | flops 1075314688 | bytes 13893632 | tf_op jit(solution)/shard_map/dot_general | solution.py:61
  55.4 1.6 exponential_multiply_fusion
  57.1 52.5 %all-reduce.2.cloned.1.call-done = bf16[4096,128]{1,0:T(8,128)(2,1)} async-done(((bf16[4096,128]{1,0:T(8,128)(2,1)}), bf16[4096,128]{1,0:T(8,128)(2,1)}) %all-reduce.2.cloned.1.call-update) | async-done | bytes 1048592 | tf_op jit(solution)/shard_map/psum | solution.py:153
  109.6 2.6 %multiply_bitcast_fusion = f32[128,4096]{0,1:T(8,128)S(1)} fusion(bf16[4096,128]{1,0:T(8,128)(2,1)} %all-reduce.2.cloned.1.call-done, f32[128]{0:T(128)S(1)} %copy-done.5, f32[4096]{0:T(1024)S(1)} %copy-done.3), kind=kLoop, calls=%fused_computation.44 | loop fusion | flops 2621440 | bytes 3162624 | tf_op jit(solution)/shard_map/transpose | solution.py:93
  112.2 1.9 copy.13
  115.8 72.6 %while.36 = (s32[]{:T(128)}, f32[4096]{0:T(1024)S(1)}, f32[4096]{0:T(1024)S(1)}, f32[16,8,4096]{2,1,0:T(8,128)S(1)}, f32[16,8,4096]{2,1,0:T(8,128)}, /*index=5*/...) while((s32[]{:T(128)}, f32[4096]{0:T(1024)S(1)}, ...), condition=%wide.region_2.3_spmd.clone, body=%wide.region_1.2_spmd.clone.sunk | while | flops 106507 | bytes 2130251 | solution.py:108
  115.8 1.6 constant_dynamic-slice_fusion.18
  117.4 1.9 constant_dynamic-slice_fusion.19
  120.5 1.6 constant_dynamic-slice_fusion.18
  122.1 1.6 constant_dynamic-slice_fusion.19
  124.9 1.6 constant_dynamic-slice_fusion.18
  126.5 1.6 constant_dynamic-slice_fusion.19
  129.3 1.8 constant_dynamic-slice_fusion.18
  131.1 1.9 constant_dynamic-slice_fusion.19
  135.8 1.6 constant_dynamic-slice_fusion.19
  140.2 1.7 constant_dynamic-slice_fusion.19
  144.6 1.6 constant_dynamic-slice_fusion.19
  147.4 1.6 constant_dynamic-slice_fusion.18
  149.0 1.6 constant_dynamic-slice_fusion.19
  151.8 1.9 constant_dynamic-slice_fusion.18
  153.7 1.6 constant_dynamic-slice_fusion.19
  158.1 1.9 constant_dynamic-slice_fusion.19
  162.7 1.6 constant_dynamic-slice_fusion.19
  165.5 1.8 constant_dynamic-slice_fusion.18
  167.3 1.6 constant_dynamic-slice_fusion.19
  171.7 1.9 constant_dynamic-slice_fusion.19
  174.8 1.6 constant_dynamic-slice_fusion.18
  176.4 1.6 constant_dynamic-slice_fusion.19
  179.2 1.8 constant_dynamic-slice_fusion.18
  181.0 1.6 constant_dynamic-slice_fusion.19
  185.4 1.9 constant_dynamic-slice_fusion.19
  188.5 1.7 fusion.10
  190.2 5.5 %all-gather = bf16[16384,1]{0,1:T(2,128)(2,1)S(1)} all-gather(bf16[4096,1]{0,1:T(2,128)(2,1)S(1)} %slice.269), channel_id=2, replica_groups=mesh['group'=2,'tm'=4,'row'=4] {'tm'}, dimensions={0}, use_global_device_ids=true | all-gather | bytes 40960 | tf_op jit(solution)/shard_map/all_gather | solution.py:12
  196.1 5.2 %all-gather.1 = bf16[16384,1]{0,1:T(2,128)(2,1)S(1)} all-gather(bf16[4096,1]{0,1:T(2,128)(2,1)S(1)} %slice.270), channel_id=3, replica_groups=mesh['group'=2,'tm'=4,'row'=4] {'tm'}, dimensions={0}, use_global_device_ids=true | all-gather | bytes 40960 | tf_op jit(solution)/shard_map/all_gather | solution.py:12
  201.7 1.9 fusion.19
  203.7 5.7 %fusion.18 = f32[1024,128]{1,0:T(8,128)S(1)} fusion(bf16[1024,4096]{1,0:T(8,128)(2,1)} %bitcast_multiply_fusion.3, f32[128,4096]{1,0:T(8,128)S(1)} %get-tuple-element.305, f32[4096]{0:T(1024)S(1)} %copy-done.4), kind=kOutput, calls=%fused_computation.70 | convolution fusion | flops 1074790400 | bytes 11026432 | tf_op jit(solution)/shard_map/dot_general | solution.py:78
  209.5 3.1 %collective-permute-start.1 = (bf16[4096,3]{0,1:T(4,128)(2,1)S(1)}, bf16[4096,3]{0,1:T(4,128)(2,1)S(1)}, u32[]{:S(2)}, u32[]{:S(2)}) collective-permute-start(bf16[4096,3]{0,1:T(4,128)(2,1)S(1)} %slice.271), channel_id=1, source_target_pairs={{0,4},{4,8},{8,12},{1,5},{5,9},{9,13},{2,6},{6,10},{10,14},{3,7},{... | collective-permute-start | bytes 73736 | tf_op jit(solution)/shard_map/ppermute | solution.py:35
  213.6 5.9 %fusion.12 = f32[1024,128]{1,0:T(8,128)S(1)} fusion(bf16[1024,4096]{1,0:T(8,128)(2,1)} %bitcast_multiply_fusion, bf16[4096,128]{0,1:T(8,128)(2,1)S(1)} %get-tuple-element.304, bf16[4096,3]{0,1:T(4,128)(2,1)S(1)} %collective-permute-done.1), kind=kOutput, calls=%fused_computation.61 | convolution fusion | flops 1075838976 | bytes 9986048 | tf_op jit(solution)/shard_map/dot_general | solution.py:78
  219.5 6.0 %convolution_add_fusion.3 = f32[1024,128]{1,0:T(8,128)S(1)} fusion(f32[1024,128]{1,0:T(8,128)S(1)} %fusion.18, bf16[1024,4096]{1,0:T(8,128)(2,1)} %bitcast_multiply_fusion.2, bf16[4096,3]{0,1:T(4,128)(2,1)S(1)} %collective-permute-done.1, bf16[4096,128]{0,1:T(8,128)(2,1)S(1)} %get-tuple-element.304), kind=kOutput, calls=%fused_computation.50 | convolution fusion | flops 1075970048 | bytes 10510336 | tf_op jit(solution)/shard_map/dot_general | solution.py:78
  225.5 3.1 %fusion.5 = bf16[1024,128]{1,0:T(8,128)(2,1)} fusion(f32[1024,128]{1,0:T(8,128)S(1)} %fusion.12, f32[1024,128]{1,0:T(8,128)S(1)} %convolution_add_fusion.3, bf16[1024,4096]{1,0:T(8,128)(2,1)S(1)} %bitcast.172, bf16[4096,3]{0,1:T(4,128)(2,1)S(1)} %collective-permute-done.1, bf16[4096,128]{0,1:T(8,128)(2,1)S(1)} %get-tuple-element.304), kind=kOutput, calls=%fused_computation.51 | convolution fusion | flops 1076232192 | bytes 10772480 | tf_op jit(solution)/shard_map/dot_general | solution.py:78
  (130 shorter events, 34.8 us)
Async XLA Ops:
  7.2 102.4 %all-reduce.2.cloned.1.call-start = ((), (), s32[]{:S(2)}) async-start(), calls=%async_computation | async-start | bytes 2097152 | tf_op jit(solution)/shard_map/psum | solution.py:153
  7.2 39.1 %collective-permute-start = (bf16[1024,3]{1,0:T(8,128)(2,1)}, bf16[1024,3]{1,0:T(8,128)(2,1)S(1)}, u32[]{:S(2)}, u32[]{:S(2)}) collective-permute-start(bf16[1024,3]{1,0:T(8,128)(2,1)} %bitcast.208), channel_id=1, source_target_pairs={{4,0},{8,4},{12,8},{5,1},{9,5},{13,9},{6,2},{10,6},{14,10},{7,3},{... | collective-permute-start | bytes 18440 | tf_op jit(solution)/shard_map/ppermute | solution.py:35
  10.7 8.1 %copy-start.2 = (s32[4096]{0:T(1024)S(1)}, s32[4096]{0:T(1024)}, u32[]{:S(2)}) copy-start(s32[4096]{0:T(1024)} %param.15) | copy-start | bytes 49156
  33.1 7.2 %copy-start.1 = (bf16[1024,128]{1,0:T(8,128)(2,1)S(1)}, bf16[1024,128]{1,0:T(8,128)(2,1)}, u32[]{:S(2)}) copy-start(bf16[1024,128]{1,0:T(8,128)(2,1)} %param.12) | copy-start | bytes 786436
  40.3 6.1 %copy-start = (bf16[1024,4096]{1,0:T(8,128)(2,1)S(1)}, bf16[1024,4096]{1,0:T(8,128)(2,1)}, u32[]{:S(2)}) copy-start(bf16[1024,4096]{1,0:T(8,128)(2,1)} %bitcast_multiply_fusion) | copy-start | bytes 25165828
  40.3 8.7 %slice-start = ((s8[8388608]{0:T(1024)(128)(4,1)}), s8[4194304]{0:T(1024)(128)(4,1)S(1)}, s32[]{:S(2)}) async-start(s8[8388608]{0:T(1024)(128)(4,1)} %bitcast.167), calls=%async_computation.1 | async-start | bytes 8388608
  46.3 2.7 %slice-start.1 = ((s8[8388608]{0:T(1024)(128)(4,1)}), s8[4194304]{0:T(1024)(128)(4,1)S(1)}, s32[]{:S(2)}) async-start(s8[8388608]{0:T(1024)(128)(4,1)} %bitcast.167), calls=%async_computation.2 | async-start | bytes 8388608
  46.4 5.2 %slice-start.2 = ((s8[8388608]{0:T(1024)(128)(4,1)}), s8[4194304]{0:T(1024)(128)(4,1)S(1)}, s32[]{:S(2)}) async-start(s8[8388608]{0:T(1024)(128)(4,1)} %bitcast.169), calls=%async_computation.3 | async-start | bytes 8388608
  49.0 2.6 %slice-start.3 = ((s8[8388608]{0:T(1024)(128)(4,1)}), s8[4194304]{0:T(1024)(128)(4,1)S(1)}, s32[]{:S(2)}) async-start(s8[8388608]{0:T(1024)(128)(4,1)} %bitcast.169), calls=%async_computation.4 | async-start | bytes 8388608
  51.6 3.6 %copy-start.5 = (f32[128]{0:T(128)S(1)}, f32[128]{0:T(128)}, u32[]{:S(2)}) copy-start(f32[128]{0:T(128)} %param.17) | copy-start | bytes 1540
  51.6 3.7 %copy-start.6 = (f32[128]{0:T(128)S(1)}, f32[128]{0:T(128)}, u32[]{:S(2)}) copy-start(f32[128]{0:T(128)} %param.18) | copy-start | bytes 1540
  51.6 3.8 %copy-start.3 = (f32[4096]{0:T(1024)S(1)}, f32[4096]{0:T(1024)}, u32[]{:S(2)}) copy-start(f32[4096]{0:T(1024)} %param.16) | copy-start | bytes 49156
  195.9 5.8 %copy-start.4 = (f32[4096]{0:T(1024)S(1)}, f32[4096]{0:T(1024)}, u32[]{:S(2)}) copy-start(f32[4096]{0:T(1024)} %param.19) | copy-start | bytes 49156
  209.5 4.1 %collective-permute-start.1 = (bf16[4096,3]{0,1:T(4,128)(2,1)S(1)}, bf16[4096,3]{0,1:T(4,128)(2,1)S(1)}, u32[]{:S(2)}, u32[]{:S(2)}) collective-permute-start(bf16[4096,3]{0,1:T(4,128)(2,1)S(1)} %slice.271), channel_id=1, source_target_pairs={{0,4},{4,8},{8,12},{1,5},{5,9},{9,13},{2,6},{6,10},{10,14},{3,7},{... | collective-permute-start | bytes 73736 | tf_op jit(solution)/shard_map/ppermute | solution.py:35
  213.6 11.9 %slice-start.4 = ((s8[8388608]{0:T(1024)(128)(4,1)}), s8[4194304]{0:T(1024)(128)(4,1)S(1)}, s32[]{:S(2)}) async-start(s8[8388608]{0:T(1024)(128)(4,1)} %bitcast.171), calls=%async_computation.5 | async-start | bytes 8388608
  219.5 6.0 %slice-start.5 = ((s8[8388608]{0:T(1024)(128)(4,1)}), s8[4194304]{0:T(1024)(128)(4,1)S(1)}, s32[]{:S(2)}) async-start(s8[8388608]{0:T(1024)(128)(4,1)} %bitcast.171), calls=%async_computation.6 | async-start | bytes 8388608
Sparse Core Ops, SparseCore 0:
  55.4 54.2 all-reduce.1
where the time goes:
time: 237 us; the launch traced here: 235 us
  local copies, waits for them, and re-layouts  77 us (32%)
  matrix products  64.9 us (27%)
  waiting for transfers between devices  52.5 us (22%)
  between operations  14.4 us (6%)
  blocking collectives  10.8 us (5%)
  other arithmetic  10.2 us (4%)
  starting transfers between devices  5.08 us (2%)
    psum x1, waiting for transfers between devices, local(): lax.psum(correlate(kernels, extended).astype(jnp.bfloat16), 'row')  52.5 us
    dot_general x4, matrix products, lag_kernels(): jnp.dot(picked.astype(jnp.bfloat16), column_onehot, preferred_element_typ...  29.6 us
    slice x16, local copies, waits for them, and re-layouts, advance(): kept_now = keep_block[inner] * kept_now  27.4 us
    slice x16, local copies, waits for them, and re-layouts, advance(): state_now = keep_block[inner] * state_now + inflow_block[inner]  26.7 us
    dot_general x4, matrix products, reconstruct(): jnp.dot(columns, extended[:, offset:offset + length], preferred_element_t...  20.7 us
    dot_general x4, matrix products, correlate(): lax.dot_general(columns, extended[:, lag_index:lag_index + length], (((0,...  14.6 us
    all_gather x2, blocking collectives, carried_in(): lax.all_gather(a.astype(kind), axis)  10.8 us
    dynamic_update_slice x16, local copies, waits for them, and re-layouts, block_recurrence(): lax.scan(advance, start, (keep_rows, inflow_rows), reverse=True)  10.7 us
  transfers between devices with their start and end apart: 3, of which 1 were waited for; matrix products, arithmetic and copies ran while one was open for 17% of the time, Pallas kernels for 0%

commit v1 on v0

--- a/solution.py
+++ b/solution.py
@@ -2,6 +2,12 @@
 import jax.numpy as jnp
 from jax import lax
 from jax.sharding import PartitionSpec as P
+
+
+def gather_and_add(array, name):
+    parts = lax.all_gather(array, name, axis=0, tiled=False)
+    acc = parts.sum(axis=0)
+    return acc
 
 
 def carried_in(array, axis, join, neutral):
@@ -150,9 +156,9 @@
     trailing = from_behind(traces[:, : number_of_lags - 1], "tm", -1)
     extended = jnp.concatenate([traces, trailing], 1)
     empty = jnp.zeros((local_rows, length), jnp.float32)
-    adjoint_total_sum = lax.psum(correlate(kernels, extended).astype(jnp.bfloat16), "row").astype(
-        jnp.float32
-    )
+    adjoint_total_sum = gather_and_add(
+        correlate(kernels, extended).astype(jnp.bfloat16), "row"
+    ).astype(jnp.float32)
     adj_state, driving = forward_step(
         adjoint_total_sum,
         element_damping_rate,

time: 237 us -> 270 us (1.14)
  waiting for transfers between devices: 52.5 us -> 81.3 us
  other arithmetic: 10.2 us -> 12.9 us
    all_gather x0 -> x1, waiting for transfers between devices: none -> 81.2 us  [gather_and_add(): parts = lax.all_gather(array, name, axis=0, tiled=False)]
    psum x1 -> x0, waiting for transfers between devices: 52.5 us -> none  [local(): lax.psum(correlate(kernels, extended).astype(jnp.bfloat16), 'row')]
    reduce_sum x0 -> x1, other arithmetic: none -> 3.47 us  [gather_and_add(): acc = parts.sum(axis=0)]
  transfers between devices with their start and end apart: 3 -> 3, of which waited for: 1 -> 1; matrix products, arithmetic and copies ran while one was open for 17% -> 15% of each run, Pallas kernels for 0% -> 0%
where the time goes in v1:
time: 270 us; the launch traced here: 269 us
  waiting for transfers between devices  81.3 us (30%)
  local copies, waits for them, and re-layouts  77.3 us (29%)
  matrix products  66.2 us (25%)
  between operations  14.4 us (5%)
  other arithmetic  12.9 us (5%)
  blocking collectives  11 us (4%)
  starting transfers between devices  5.38 us (2%)
    all_gather x1, waiting for transfers between devices, gather_and_add(): parts = lax.all_gather(array, name, axis=0, tiled=False)  81.2 us
    dot_general x4, matrix products, lag_kernels(): jnp.dot(picked.astype(jnp.bfloat16), column_onehot, preferred_element_typ...  30.9 us
    slice x16, local copies, waits for them, and re-layouts, advance(): kept_now = keep_block[inner] * kept_now  27.3 us
    slice x16, local copies, waits for them, and re-layouts, advance(): state_now = keep_block[inner] * state_now + inflow_block[inner]  27.1 us
    dot_general x4, matrix products, reconstruct(): jnp.dot(columns, extended[:, offset:offset + length], preferred_element_t...  20.7 us
    dot_general x4, matrix products, correlate(): lax.dot_general(columns, extended[:, lag_index:lag_index + length], (((0,...  14.6 us
    all_gather x2, blocking collectives, carried_in(): lax.all_gather(a.astype(kind), axis)  11 us
    dynamic_update_slice x16, local copies, waits for them, and re-layouts, block_recurrence(): lax.scan(advance, start, (keep_rows, inflow_rows), reverse=True)  10.7 us
  transfers between devices with their start and end apart: 3, of which 1 were waited for; matrix products, arithmetic and copies ran while one was open for 15% of the time, Pallas kernels for 0%

profile of v1, /device:TPU:1, one launch (start us, length us, event | category | flops | bytes accessed | tf_op | source)
XLA Modules:
  0.0 269.0 jit_solution(10388991343638829372)
XLA Ops:
  7.2 2.0 collective-permute-start
  10.7 8.4 %bitcast_multiply_fusion.3 = bf16[1024,4096]{1,0:T(8,128)(2,1)} fusion(bf16[4,1024,4096]{2,1,0:T(8,128)(2,1)} %param.13, s32[4096]{0:T(1024)} %param.15, s32[1024]{0:T(1024)S(1)} %dynamic_slice.40, bf16[4,32,32]{2,1,0:T(8,128)(2,1)S(1)} %convert.16), kind=kOutput, calls=%fused_computation.34 | convolution fusion | flops 291700736 | bytes 16805888 | tf_op jit(solution)/shard_map/dot_general | solution.py:55
  19.1 7.5 %bitcast_multiply_fusion.2 = bf16[1024,4096]{1,0:T(8,128)(2,1)} fusion(bf16[4,1024,4096]{2,1,0:T(8,128)(2,1)} %param.13, s32[4096]{0:T(1024)S(1)} %copy-done.2, s32[1024]{0:T(1024)S(1)} %dynamic_slice.40, bf16[4,32,32]{2,1,0:T(8,128)(2,1)S(1)} %convert.16), kind=kOutput, calls=%fused_computation.33 | convolution fusion | flops 291700736 | bytes 16805888 | tf_op jit(solution)/shard_map/dot_general | solution.py:55
  26.6 7.4 %bitcast_multiply_fusion = bf16[1024,4096]{1,0:T(8,128)(2,1)} fusion(bf16[4,1024,4096]{2,1,0:T(8,128)(2,1)} %param.13, s32[4096]{0:T(1024)S(1)} %copy-done.2, s32[1024]{0:T(1024)S(1)} %dynamic_slice.40, bf16[4,32,32]{2,1,0:T(8,128)(2,1)S(1)} %convert.16), kind=kOutput, calls=%fused_computation.31 | convolution fusion | flops 291700736 | bytes 16805888 | tf_op jit(solution)/shard_map/dot_general | solution.py:55
  34.1 7.5 %bitcast_multiply_fusion.1 = bf16[1024,4096]{1,0:T(8,128)(2,1)} fusion(bf16[4,1024,4096]{2,1,0:T(8,128)(2,1)} %param.13, s32[4096]{0:T(1024)S(1)} %copy-done.2, s32[1024]{0:T(1024)S(1)} %dynamic_slice.40, bf16[4,32,32]{2,1,0:T(8,128)(2,1)S(1)} %convert.16), kind=kOutput, calls=%fused_computation.32 | convolution fusion | flops 291700736 | bytes 16805888 | tf_op jit(solution)/shard_map/dot_general | solution.py:55
  41.6 6.0 %fusion.42 = f32[4096,128]{1,0:T(8,128)S(1)} fusion(bf16[1024,4096]{1,0:T(8,128)(2,1)} %bitcast_multiply_fusion.3, bf16[1024,128]{1,0:T(8,128)(2,1)S(1)} %copy-done.1), kind=kOutput, calls=%fused_computation.94 | convolution fusion | flops 1073741824 | bytes 10747904 | tf_op jit(solution)/shard_map/dot_general | solution.py:67
  47.7 2.6 fusion.20
  50.3 2.5 convolution_add_fusion.1
  53.0 3.5 %fusion.2 = bf16[4096,128]{1,0:T(8,128)(2,1)} fusion(f32[4096,128]{1,0:T(8,128)S(1)} %fusion.20, f32[4096,128]{1,0:T(8,128)S(1)} %convolution_add_fusion.1, bf16[1024,4096]{1,0:T(8,128)(2,1)S(1)} %bitcast.171, bf16[1024,131]{1,0:T(8,128)(2,1)S(1)} %constant_dynamic-update-slice_fusion), kind=kOutput, calls=%fused_computation.38 | convolution fusion | flops 1075314688 | bytes 13893632 | tf_op jit(solution)/shard_map/dot_general | solution.py:67
  56.7 1.7 exponential_multiply_fusion
  58.4 81.2 %all-gather.5.cloned.1.call-done = bf16[16384,128]{1,0:T(8,128)(2,1)} async-done(((bf16[4096,128]{1,0:T(8,128)(2,1)}), bf16[16384,128]{1,0:T(8,128)(2,1)}) %all-gather.5.cloned.1.call-update) | async-done | bytes 4194320 | tf_op jit(solution)/shard_map/all_gather | solution.py:8
  139.6 3.5 %reduce_sum.12 = bf16[4096,128]{1,0:T(8,128)(2,1)S(1)} reduce(bf16[4,4096,128]{2,1,0:T(8,128)(2,1)} %bitcast.174, bf16[]{:T(256)} %constant.91.clone.1), dimensions={0}, to_apply=%region_0.0 | reduce | flops 1572864 | bytes 5242882 | tf_op jit(solution)/shard_map/reduce_sum | solution.py:9
  143.1 1.8 bitcast_multiply_fusion.5
  144.9 1.8 copy.15
  146.9 1.6 broadcast.30.clone
  148.5 73.0 %while.36 = (s32[]{:T(128)}, f32[4096]{0:T(1024)S(1)}, f32[4096]{0:T(1024)S(1)}, f32[16,8,4096]{2,1,0:T(8,128)S(1)}, f32[16,8,4096]{2,1,0:T(8,128)}, /*index=5*/...) while((s32[]{:T(128)}, f32[4096]{0:T(1024)S(1)}, ...), condition=%wide.region_2.3_spmd.clone, body=%wide.region_1.2_spmd.clone.sunk | while | flops 106507 | bytes 2130251 | solution.py:114
  148.5 1.9 constant_dynamic-slice_fusion.18
  150.4 1.7 constant_dynamic-slice_fusion.19
  154.8 1.9 constant_dynamic-slice_fusion.19
  157.9 1.6 constant_dynamic-slice_fusion.18
  159.5 1.6 constant_dynamic-slice_fusion.19
  162.3 1.9 constant_dynamic-slice_fusion.18
  164.2 1.9 constant_dynamic-slice_fusion.19
  168.8 1.6 constant_dynamic-slice_fusion.19
  171.6 1.6 constant_dynamic-slice_fusion.18
  173.2 1.6 constant_dynamic-slice_fusion.19
  177.6 1.6 constant_dynamic-slice_fusion.19
  180.4 1.6 constant_dynamic-slice_fusion.18
  182.0 1.9 constant_dynamic-slice_fusion.19
  189.4 1.9 constant_dynamic-slice_fusion.18
  191.2 1.6 constant_dynamic-slice_fusion.19
  195.6 1.6 constant_dynamic-slice_fusion.19
  200.0 1.6 constant_dynamic-slice_fusion.19
  202.8 1.9 constant_dynamic-slice_fusion.18
  204.7 1.9 constant_dynamic-slice_fusion.19
  207.8 1.6 constant_dynamic-slice_fusion.18
  209.4 1.9 constant_dynamic-slice_fusion.19
  214.0 1.6 constant_dynamic-slice_fusion.19
  216.8 1.9 constant_dynamic-slice_fusion.18
  221.5 1.7 fusion.10
  223.2 5.7 %all-gather.1 = bf16[16384,1]{0,1:T(2,128)(2,1)S(1)} all-gather(bf16[4096,1]{0,1:T(2,128)(2,1)S(1)} %slice.269), channel_id=3, replica_groups=mesh['group'=2,'tm'=4,'row'=4] {'tm'}, dimensions={0}, use_global_device_ids=true | all-gather | bytes 40960 | tf_op jit(solution)/shard_map/all_gather | solution.py:18
  229.3 5.2 %all-gather.2 = bf16[16384,1]{0,1:T(2,128)(2,1)S(1)} all-gather(bf16[4096,1]{0,1:T(2,128)(2,1)S(1)} %slice.270), channel_id=4, replica_groups=mesh['group'=2,'tm'=4,'row'=4] {'tm'}, dimensions={0}, use_global_device_ids=true | all-gather | bytes 40960 | tf_op jit(solution)/shard_map/all_gather | solution.py:18
  234.9 1.9 fusion.19
  236.9 5.7 %fusion.18 = f32[1024,128]{1,0:T(8,128)S(1)} fusion(bf16[1024,4096]{1,0:T(8,128)(2,1)} %bitcast_multiply_fusion.3, f32[128,4096]{1,0:T(8,128)S(1)} %get-tuple-element.309, f32[4096]{0:T(1024)S(1)} %copy-done.4), kind=kOutput, calls=%fused_computation.70 | convolution fusion | flops 1074790400 | bytes 11026432 | tf_op jit(solution)/shard_map/dot_general | solution.py:84
  242.7 3.4 %collective-permute-start.1 = (bf16[4096,3]{0,1:T(4,128)(2,1)S(1)}, bf16[4096,3]{0,1:T(4,128)(2,1)S(1)}, u32[]{:S(2)}, u32[]{:S(2)}) collective-permute-start(bf16[4096,3]{0,1:T(4,128)(2,1)S(1)} %slice.271), channel_id=1, source_target_pairs={{0,4},{4,8},{8,12},{1,5},{5,9},{9,13},{2,6},{6,10},{10,14},{3,7},{... | collective-permute-start | bytes 73736 | tf_op jit(solution)/shard_map/ppermute | solution.py:41
  247.1 5.9 %fusion.12 = f32[1024,128]{1,0:T(8,128)S(1)} fusion(bf16[1024,4096]{1,0:T(8,128)(2,1)} %bitcast_multiply_fusion, bf16[4096,128]{0,1:T(8,128)(2,1)S(1)} %get-tuple-element.308, bf16[4096,3]{0,1:T(4,128)(2,1)S(1)} %collective-permute-done.1), kind=kOutput, calls=%fused_computation.61 | convolution fusion | flops 1075838976 | bytes 9986048 | tf_op jit(solution)/shard_map/dot_general | solution.py:84
  253.0 6.0 %convolution_add_fusion.3 = f32[1024,128]{1,0:T(8,128)S(1)} fusion(f32[1024,128]{1,0:T(8,128)S(1)} %fusion.18, bf16[1024,4096]{1,0:T(8,128)(2,1)} %bitcast_multiply_fusion.2, bf16[4096,3]{0,1:T(4,128)(2,1)S(1)} %collective-permute-done.1, bf16[4096,128]{0,1:T(8,128)(2,1)S(1)} %get-tuple-element.308), kind=kOutput, calls=%fused_computation.50 | convolution fusion | flops 1075970048 | bytes 10510336 | tf_op jit(solution)/shard_map/dot_general | solution.py:84
  259.0 3.1 %fusion.5 = bf16[1024,128]{1,0:T(8,128)(2,1)} fusion(f32[1024,128]{1,0:T(8,128)S(1)} %fusion.12, f32[1024,128]{1,0:T(8,128)S(1)} %convolution_add_fusion.3, bf16[1024,4096]{1,0:T(8,128)(2,1)S(1)} %bitcast.173, bf16[4096,3]{0,1:T(4,128)(2,1)S(1)} %collective-permute-done.1, bf16[4096,128]{0,1:T(8,128)(2,1)S(1)} %get-tuple-element.308), kind=kOutput, calls=%fused_computation.51 | convolution fusion | flops 1076232192 | bytes 10772480 | tf_op jit(solution)/shard_map/dot_general | solution.py:84
  (131 shorter events, 36.4 us)
Async XLA Ops:
  7.2 132.5 %all-gather.5.cloned.1.call-start = ((), (), s32[]{:S(2)}) async-start(), calls=%async_computation | async-start | bytes 5242880 | tf_op jit(solution)/shard_map/all_gather | solution.py:8
  7.2 40.4 %collective-permute-start = (bf16[1024,3]{1,0:T(8,128)(2,1)}, bf16[1024,3]{1,0:T(8,128)(2,1)S(1)}, u32[]{:S(2)}, u32[]{:S(2)}) collective-permute-start(bf16[1024,3]{1,0:T(8,128)(2,1)} %bitcast.210), channel_id=1, source_target_pairs={{4,0},{8,4},{12,8},{5,1},{9,5},{13,9},{6,2},{10,6},{14,10},{7,3},{... | collective-permute-start | bytes 18440 | tf_op jit(solution)/shard_map/ppermute | solution.py:41
  10.7 8.4 %copy-start.2 = (s32[4096]{0:T(1024)S(1)}, s32[4096]{0:T(1024)}, u32[]{:S(2)}) copy-start(s32[4096]{0:T(1024)} %param.15) | copy-start | bytes 49156
  34.1 7.5 %copy-start.1 = (bf16[1024,128]{1,0:T(8,128)(2,1)S(1)}, bf16[1024,128]{1,0:T(8,128)(2,1)}, u32[]{:S(2)}) copy-start(bf16[1024,128]{1,0:T(8,128)(2,1)} %param.12) | copy-start | bytes 786436
  41.6 6.1 %copy-start = (bf16[1024,4096]{1,0:T(8,128)(2,1)S(1)}, bf16[1024,4096]{1,0:T(8,128)(2,1)}, u32[]{:S(2)}) copy-start(bf16[1024,4096]{1,0:T(8,128)(2,1)} %bitcast_multiply_fusion) | copy-start | bytes 25165828
  41.6 8.7 %slice-start = ((s8[8388608]{0:T(1024)(128)(4,1)}), s8[4194304]{0:T(1024)(128)(4,1)S(1)}, s32[]{:S(2)}) async-start(s8[8388608]{0:T(1024)(128)(4,1)} %bitcast.168), calls=%async_computation.1 | async-start | bytes 8388608
  47.6 2.7 %slice-start.1 = ((s8[8388608]{0:T(1024)(128)(4,1)}), s8[4194304]{0:T(1024)(128)(4,1)S(1)}, s32[]{:S(2)}) async-start(s8[8388608]{0:T(1024)(128)(4,1)} %bitcast.168), calls=%async_computation.2 | async-start | bytes 8388608
  47.7 5.2 %slice-start.2 = ((s8[8388608]{0:T(1024)(128)(4,1)}), s8[4194304]{0:T(1024)(128)(4,1)S(1)}, s32[]{:S(2)}) async-start(s8[8388608]{0:T(1024)(128)(4,1)} %bitcast.170), calls=%async_computation.3 | async-start | bytes 8388608
  50.3 2.6 slice-start.3
  52.9 3.6 %copy-start.5 = (f32[128]{0:T(128)S(1)}, f32[128]{0:T(128)}, u32[]{:S(2)}) copy-start(f32[128]{0:T(128)} %param.17) | copy-start | bytes 1540
  52.9 3.7 %copy-start.6 = (f32[128]{0:T(128)S(1)}, f32[128]{0:T(128)}, u32[]{:S(2)}) copy-start(f32[128]{0:T(128)} %param.18) | copy-start | bytes 1540
  52.9 3.8 %copy-start.3 = (f32[4096]{0:T(1024)S(1)}, f32[4096]{0:T(1024)}, u32[]{:S(2)}) copy-start(f32[4096]{0:T(1024)} %param.16) | copy-start | bytes 49156
  229.1 5.8 %copy-start.4 = (f32[4096]{0:T(1024)S(1)}, f32[4096]{0:T(1024)}, u32[]{:S(2)}) copy-start(f32[4096]{0:T(1024)} %param.19) | copy-start | bytes 49156
  242.7 4.4 %collective-permute-start.1 = (bf16[4096,3]{0,1:T(4,128)(2,1)S(1)}, bf16[4096,3]{0,1:T(4,128)(2,1)S(1)}, u32[]{:S(2)}, u32[]{:S(2)}) collective-permute-start(bf16[4096,3]{0,1:T(4,128)(2,1)S(1)} %slice.271), channel_id=1, source_target_pairs={{0,4},{4,8},{8,12},{1,5},{5,9},{9,13},{2,6},{6,10},{10,14},{3,7},{... | collective-permute-start | bytes 73736 | tf_op jit(solution)/shard_map/ppermute | solution.py:41
  247.1 11.9 %slice-start.4 = ((s8[8388608]{0:T(1024)(128)(4,1)}), s8[4194304]{0:T(1024)(128)(4,1)S(1)}, s32[]{:S(2)}) async-start(s8[8388608]{0:T(1024)(128)(4,1)} %bitcast.172), calls=%async_computation.5 | async-start | bytes 8388608
  253.0 6.0 %slice-start.5 = ((s8[8388608]{0:T(1024)(128)(4,1)}), s8[4194304]{0:T(1024)(128)(4,1)S(1)}, s32[]{:S(2)}) async-start(s8[8388608]{0:T(1024)(128)(4,1)} %bitcast.172), calls=%async_computation.6 | async-start | bytes 8388608
Sparse Core Ops, SparseCore 0:
  56.6 82.9 all-gather.4
